TPU v7x, 512 devices: a whole 4x4x16 slice. The times are simulated.
512 devices in a mesh: seq: 128 (over z, x, core), dp: 4 (over y).
Axes of the slice: x: 4, y: 4, z: 16, core: 2. Of those that a mesh axis runs over, the one named last changes fastest.
Arguments:
- queries: bfloat16 [8192, 512], P(('dp', 'seq')), parts along dimension 0, may hold values from -6 to 6
- keys: bfloat16 [8192, 512], P(('dp', 'seq')), parts along dimension 0, may hold values from -6 to 6
- values: bfloat16 [8192, 512], P(('dp', 'seq')), parts along dimension 0, may hold values from -6 to 6
- residual: bfloat16 [8192, 1024], P(('dp', 'seq')), parts along dimension 0, may hold values from -16 to 16
- lengths: int32 [4], P('dp'), parts along dimension 0, may hold values from 1024 to 2048
- out_proj: bfloat16 [512, 1024], replicated, may hold values from -0.75 to 0.75
- ln_gain: float32 [1024], replicated, may hold values from 0.1 to 1.9
- ln_bias: float32 [1024], replicated, may hold values from -3 to 3
- conv_in: bfloat16 [1024, 1024], replicated, may hold values from -0.1875 to 0.1875
- taps: float32 [31, 512], replicated, may hold values from -1 to 1
- bn_scale: float32 [512], replicated, may hold values from 0.5 to 2
- bn_shift: float32 [512], replicated, may hold values from -3 to 3
- conv_out: bfloat16 [512, 1024], replicated, may hold values from -0.25 to 0.25
Outputs:
- block_out: bfloat16 [8192, 1024], P(('dp', 'seq')), parts along dimension 0
There are 4 independent parts, one for each index of `dp`. A program takes and returns all parts, laid end to end along the dimension named above; an argument that names none is the same for every part. Nothing has to cross between parts.
All inputs are finite; a program needn't handle non-finite values.
Results may differ from a plain program's by a relative error of at most 0.0075.
Values may be sent and summed in bfloat16 or wider, within the bound.
A program may use at most 64 MiB of HBM per device.

v0:
```python
import math
import jax
import jax.numpy as jnp
from jax import lax
from jax.sharding import PartitionSpec as P

HEAD_DIM = 64


def extended(block, sides, width):
    for axis, dim in sides:
        count = lax.axis_size(axis)
        forward = [(i, i + 1) for i in range(count - 1)]
        backward = [(target, source) for source, target in forward]
        low = lax.ppermute(
            lax.slice_in_dim(block, block.shape[dim] - width, None, axis=dim), axis, forward
        )
        high = lax.ppermute(lax.slice_in_dim(block, 0, width, axis=dim), axis, backward)
        block = jnp.concatenate([low, block, high], axis=dim)
    return block


def norm_lift(rows, row_frames, limit, ln_gain, ln_bias, conv_in):
    average = jnp.mean(rows, axis=-1, keepdims=True)
    centred = rows - average
    variance = jnp.mean(centred * centred, axis=-1, keepdims=True)
    normed = (centred * lax.rsqrt(variance + 1e-05) * ln_gain + ln_bias).astype(jnp.bfloat16)
    lifted = jnp.dot(normed, conv_in, preferred_element_type=jnp.float32)
    channels = conv_in.shape[1] // 2
    inside = ((row_frames >= 0) & (row_frames < limit)).astype(jnp.float32)
    return (inside[:, None] * lifted[:, :channels] * jax.nn.sigmoid(lifted[:, channels:])).astype(
        jnp.bfloat16
    )


def attend(carried, query_rows, key_block, value_block, key_frames, limit):
    running, totals, weighted = carried
    factor = 1.0 / math.sqrt(query_rows.shape[2])
    scores = (
        jnp.einsum("qhd,khd->hqk", query_rows, key_block, preferred_element_type=jnp.float32)
        * factor
    )
    scores = jnp.where((key_frames < limit)[None, None, :], scores, -1e30)
    highest = jnp.maximum(running, jnp.max(scores, axis=-1))
    rescale = jnp.exp(running - highest)
    powered = jnp.exp(scores - highest[:, :, None])
    totals = totals * rescale + jnp.sum(powered, axis=-1)
    weighted = weighted * jnp.transpose(rescale)[:, :, None] + jnp.einsum(
        "hqk,khd->qhd",
        powered.astype(jnp.bfloat16),
        value_block,
        preferred_element_type=jnp.float32,
    )
    return (highest, totals, weighted)


def split_pair(packed, columns, heads_here):
    row_count = packed.shape[0]
    key_part = packed[:, 0, :columns].reshape(row_count, heads_here, columns // heads_here)
    value_part = packed[:, 0, columns:].reshape(row_count, heads_here, columns // heads_here)
    return (key_part, value_part)


def on_device(
    queries,
    keys,
    values,
    residual,
    lengths,
    out_proj,
    ln_gain,
    ln_bias,
    conv_in,
    taps,
    bn_scale,
    bn_shift,
    conv_out,
):
    frames_here = residual.shape[0]
    width_att = queries.shape[1]
    devices = lax.axis_size("seq")
    position = lax.axis_index("seq")
    heads_all = width_att // HEAD_DIM
    groups = min(devices, heads_all)
    copies = devices // groups
    heads_here = heads_all // groups
    columns = heads_here * HEAD_DIM
    sub_rows = frames_here // copies
    query_count = devices * sub_rows
    limit = lengths[0]
    local_frames = position * frames_here + jnp.arange(frames_here, dtype=jnp.int32)
    valid_local = (local_frames < limit).astype(jnp.float32)
    query_rows = lax.all_to_all(
        queries.reshape(sub_rows, devices, columns), "seq", split_axis=1, concat_axis=0, tiled=True
    )
    carried = (
        jnp.full((heads_here, query_count), -1e30, jnp.float32),
        jnp.zeros((heads_here, query_count), jnp.float32),
        jnp.zeros((query_count, heads_here, HEAD_DIM), jnp.float32),
    )
    paired = jnp.concatenate(
        [
            keys.reshape(frames_here, 1, groups, columns),
            values.reshape(frames_here, 1, groups, columns),
        ],
        axis=3,
    )
    paired = jnp.broadcast_to(paired, (frames_here, copies, groups, 2 * columns)).reshape(
        frames_here, devices, 2 * columns
    )
    all_pairs = lax.all_to_all(paired, "seq", split_axis=1, concat_axis=0, tiled=True)
    block_size = groups * frames_here
    block_count = (limit + block_size - 1) // block_size

    def visit(number, looped):
        start = number * block_size
        current = lax.dynamic_slice_in_dim(all_pairs, start, block_size, 0)
        key_block, value_block = split_pair(current, columns, heads_here)
        key_frames = start + jnp.arange(block_size, dtype=jnp.int32)
        return attend(looped, query_rows, key_block, value_block, key_frames, limit)

    carried = lax.fori_loop(0, block_count, visit, carried)
    running, totals, weighted = carried
    context = (weighted / jnp.transpose(totals)[:, :, None]).astype(jnp.bfloat16)
    returned = lax.all_to_all(
        context.reshape(devices, sub_rows, 1, columns),
        "seq",
        split_axis=0,
        concat_axis=2,
        tiled=True,
    )
    context_here = returned.reshape(frames_here, width_att)
    mixed = residual.astype(jnp.float32) + valid_local[:, None] * jnp.dot(
        context_here, out_proj, preferred_element_type=jnp.float32
    )
    margin = taps.shape[0] // 2
    gated = norm_lift(mixed, local_frames, limit, ln_gain, ln_bias, conv_in)
    widened = extended(gated, (("seq", 0),), margin)
    widened = widened.astype(jnp.float32)
    filtered = taps[0] * widened[0:frames_here]
    for offset in range(1, taps.shape[0]):
        filtered = filtered + taps[offset] * widened[offset : offset + frames_here]
    shifted = filtered * bn_scale + bn_shift
    activated = (shifted * jax.nn.sigmoid(shifted)).astype(jnp.bfloat16)
    return (mixed + jnp.dot(activated, conv_out, preferred_element_type=jnp.float32)).astype(
        jnp.bfloat16
    )


def solution(mesh):
    placed = (
        P(("dp", "seq"), None),
        P(("dp", "seq"), None),
        P(("dp", "seq"), None),
        P(("dp", "seq"), None),
        P("dp"),
        P(),
        P(),
        P(),
        P(),
        P(),
        P(),
        P(),
        P(),
    )
    return jax.shard_map(
        on_device, mesh=mesh, in_specs=placed, out_specs=P(("dp", "seq"), None), check_vma=False
    )
```

profile of v0, /device:TPU:31, one launch (start us, length us, event | category | flops | bytes accessed | tf_op | source)
XLA Modules:
  0.0 132.5 jit_solution(11860965346838346635)
XLA Ops:
  0.0 1.6 %reshape.94 = bf16[1,128,64]{2,0,1:T(2,128)(2,1)} reshape(bf16[16,512]{1,0:T(8,128)(2,1)} %param.15) | data formatting | bytes 32768 | tf_op jit(solution)/shard_map/reshape | solution.py:94
  1.6 19.7 %all-to-all-start.1 = ((bf16[1,128,64]{2,0,1:T(2,128)(2,1)}), bf16[1,128,64]{2,0,1:T(2,128)(2,1)S(1)}, u32[]{:S(2)}, u32[]{:S(2)}) async-start(bf16[1,128,64]{2,0,1:T(2,128)(2,1)} %reshape.94), calls=%async_computation.1 | async-start | bytes 131072 | tf_op jit(solution)/shard_map/all_to_all | solution.py:93
  21.3 0.8 reshape.88
  22.1 0.8 reshape.89
  23.0 11.7 %all-to-all-done.1 = bf16[1,128,64]{2,0,1:T(2,128)(2,1)S(1)} async-done(((bf16[1,128,64]{2,0,1:T(2,128)(2,1)}), bf16[1,128,64]{2,0,1:T(2,128)(2,1)S(1)}, u32[]{:S(2)}, u32[]{:S(2)}) %all-to-all-start.1) | async-done | bytes 16416 | tf_op jit(solution)/shard_map/all_to_all | solution.py:93
  34.7 0.9 broadcast_in_dim.42
  35.6 7.2 %all-to-all-start = ((bf16[16,128,128]{2,0,1:T(8,128)(2,1)}), bf16[16,128,128]{2,0,1:T(8,128)(2,1)S(1)}, u32[]{:S(2)}, u32[]{:S(2)}) async-start(bf16[16,128,128]{2,0,1:T(8,128)(2,1)} %bitcast.11), calls=%async_computation | async-start | bytes 1048576 | tf_op jit(solution)/shard_map/all_to_all | solution.py:111
  43.7 32.1 %all-to-all-done = bf16[16,128,128]{2,0,1:T(8,128)(2,1)S(1)} async-done(((bf16[16,128,128]{2,0,1:T(8,128)(2,1)}), bf16[16,128,128]{2,0,1:T(8,128)(2,1)S(1)}, u32[]{:S(2)}, u32[]{:S(2)}) %all-to-all-start) | async-done | bytes 524320 | tf_op jit(solution)/shard_map/all_to_all | solution.py:111
  75.8 18.8 %while.14 = (s32[]{:T(128)}, f32[1,128]{1,0:T(1,128)S(1)}, f32[1,128]{1,0:T(1,128)S(1)}, f32[128,1,64]{0,2,1:T(8,128)S(1)}, s32[]{:T(128)}, /*index=5*/s32[]{:T(...) while((s32[]{:T(128)}, f32[1,128]{1,0:T(1,128)S(1)}, ...), condition=%wide.region_3.4_spmd, body=%wide.region_0.3_spmd.sunk | while | flops 4326023 | bytes 353099 | solution.py:122
  75.8 0.7 add_compare_fusion.2
  77.0 0.7 add_compare_fusion.2
  78.1 0.7 add_compare_fusion.2
  79.3 0.7 add_compare_fusion.2
  80.5 0.7 add_compare_fusion.2
  81.7 0.7 add_compare_fusion.2
  82.9 0.7 add_compare_fusion.2
  85.2 0.7 add_compare_fusion.2
  86.4 0.7 add_compare_fusion.2
  87.6 0.7 add_compare_fusion.2
  88.7 0.7 add_compare_fusion.2
  89.9 0.7 add_compare_fusion.2
  91.1 0.7 add_compare_fusion.2
  92.3 0.7 add_compare_fusion.2
  93.4 0.7 add_compare_fusion.2
  94.6 0.7 copy.28
  95.4 7.2 %all-to-all-start.2 = ((bf16[128,1,1,64]{3,2,1,0:T(2,128)(2,1)}), bf16[128,1,1,64]{3,2,1,0:T(2,128)(2,1)S(1)}, u32[]{:S(2)}, u32[]{:S(2)}) async-start(bf16[128,1,1,64]{3,2,1,0:T(2,128)(2,1)} %copy.28), calls=%async_computation.2 | async-start | bytes 131072 | tf_op jit(solution)/shard_map/all_to_all | solution.py:125
  102.6 13.4 %all-to-all-done.2 = bf16[128,1,1,64]{3,2,1,0:T(2,128)(2,1)S(1)} async-done(((bf16[128,1,1,64]{3,2,1,0:T(2,128)(2,1)}), bf16[128,1,1,64]{3,2,1,0:T(2,128)(2,1)S(1)}, u32[]{:S(2)}, u32[]{:S(2)}) %all-to-all-start.2) | async-done | bytes 16416 | tf_op jit(solution)/shard_map/all_to_all | solution.py:125
  116.3 1.6 %fusion.94 = (f32[16]{0:T(128)S(1)}, f32[16,1024]{1,0:T(8,128)S(1)}) fusion(bf16[16,512]{1,0:T(8,128)(2,1)S(1)} %reshape.93, bf16[512,1024]{1,0:T(8,128)(2,1)} %param.20, f32[16]{0:T(128)S(1)} %compare_convert_fusion, bf16[16,1024]{1,0:T(8,128)(2,1)S(1)} %copy-done.2), kind=kOutput, calls=%fused_computation.148 | convolution fusion | flops 16842736 | bytes 1163392 | tf_op jit(solution)/shard_map/dot_general | solution.py:133
  118.7 4.3 %collective-permute-start = (bf16[15,512]{1,0:T(8,128)(2,1)S(1)}, bf16[15,512]{1,0:T(8,128)(2,1)S(1)}, u32[]{:S(2)}, u32[]{:S(2)}) collective-permute-start(bf16[15,512]{1,0:T(8,128)(2,1)S(1)} %get-tuple-element.126), channel_id=1, source_target_pairs={{0,4},{4,8},{8,12},{12,16},{16,20},{20,24},{24,28},{28,32},{32,36}... | collective-permute-start | bytes 46088 | tf_op jit(solution)/shard_map/ppermute | solution.py:15
  123.0 1.9 %collective-permute-start.1 = (bf16[15,512]{1,0:T(8,128)(2,1)S(1)}, bf16[15,512]{1,0:T(8,128)(2,1)S(1)}, u32[]{:S(2)}, u32[]{:S(2)}) collective-permute-start(bf16[15,512]{1,0:T(8,128)(2,1)S(1)} %get-tuple-element.127), channel_id=1, source_target_pairs={{4,0},{8,4},{12,8},{16,12},{20,16},{24,20},{28,24},{32,28},{36,32}... | collective-permute-start | bytes 46088 | tf_op jit(solution)/shard_map/ppermute | solution.py:18
  125.0 5.2 %collective-permute-done.1 = bf16[15,512]{1,0:T(8,128)(2,1)S(1)} collective-permute-done((bf16[15,512]{1,0:T(8,128)(2,1)S(1)}, bf16[15,512]{1,0:T(8,128)(2,1)S(1)}, u32[]{:S(2)}, u32[]{:S(2)}) %collective-permute-start.1) | collective-permute-done | bytes 15392 | tf_op jit(solution)/shard_map/ppermute | solution.py:18
  130.2 2.3 %fusion.11 = bf16[16,1024]{1,0:T(8,128)(2,1)} fusion(f32[16,1024]{1,0:T(8,128)S(1)} %get-tuple-element.129, bf16[512,1024]{1,0:T(8,128)(2,1)} %param.27, f32[46,512]{1,0:T(8,128)S(1)} %maximum_convert_fusion, f32[512]{0:T(512)S(1)} %copy-done.5, f32[512]{0:T(512)S(1)} %copy-done.6, f32[512]{0:T(512)S(1)} %bitcast.128, f32[512]{0:T(512)S(1)} %bitcast.129, ...), kind=kOutput, calls=%fused_computation.21 | convolution fusion | flops 17367040 | bytes 2230272 | tf_op jit(solution)/shard_map/dot_general | solution.py:145
  (132 shorter events, 9.7 us)
Async XLA Ops:
  0.0 118.1 %copy-start = (bf16[1024,1024]{1,0:T(8,128)(2,1)S(1)}, bf16[1024,1024]{1,0:T(8,128)(2,1)}, u32[]{:S(2)}) copy-start(bf16[1024,1024]{1,0:T(8,128)(2,1)} %param.23) | copy-start | bytes 6291460
  0.0 43.5 %copy-start.1 = (f32[31,512]{1,0:T(8,128)S(1)}, f32[31,512]{1,0:T(8,128)}, u32[]{:S(2)}) copy-start(f32[31,512]{1,0:T(8,128)} %param.24) | copy-start | bytes 190468
  1.6 33.1 %all-to-all-start.1 = ((bf16[1,128,64]{2,0,1:T(2,128)(2,1)}), bf16[1,128,64]{2,0,1:T(2,128)(2,1)S(1)}, u32[]{:S(2)}, u32[]{:S(2)}) async-start(bf16[1,128,64]{2,0,1:T(2,128)(2,1)} %reshape.94), calls=%async_computation.1 | async-start | bytes 131072 | tf_op jit(solution)/shard_map/all_to_all | solution.py:93
  23.0 93.3 %copy-start.2 = (bf16[16,1024]{1,0:T(8,128)(2,1)S(1)}, bf16[16,1024]{1,0:T(8,128)(2,1)}, u32[]{:S(2)}) copy-start(bf16[16,1024]{1,0:T(8,128)(2,1)} %param.18) | copy-start | bytes 98308
  35.6 40.2 %all-to-all-start = ((bf16[16,128,128]{2,0,1:T(8,128)(2,1)}), bf16[16,128,128]{2,0,1:T(8,128)(2,1)S(1)}, u32[]{:S(2)}, u32[]{:S(2)}) async-start(bf16[16,128,128]{2,0,1:T(8,128)(2,1)} %bitcast.11), calls=%async_computation | async-start | bytes 1048576 | tf_op jit(solution)/shard_map/all_to_all | solution.py:111
  42.8 75.3 %copy-start.3 = (f32[1024]{0:T(1024)S(1)}, f32[1024]{0:T(1024)}, u32[]{:S(2)}) copy-start(f32[1024]{0:T(1024)} %param.22) | copy-start | bytes 12292
  42.8 75.3 %copy-start.4 = (f32[1024]{0:T(1024)S(1)}, f32[1024]{0:T(1024)}, u32[]{:S(2)}) copy-start(f32[1024]{0:T(1024)} %param.21) | copy-start | bytes 12292
  95.4 34.8 %copy-start.5 = (f32[512]{0:T(512)S(1)}, f32[512]{0:T(512)}, u32[]{:S(2)}) copy-start(f32[512]{0:T(512)} %param.26) | copy-start | bytes 6148
  95.4 34.8 %copy-start.6 = (f32[512]{0:T(512)S(1)}, f32[512]{0:T(512)}, u32[]{:S(2)}) copy-start(f32[512]{0:T(512)} %param.25) | copy-start | bytes 6148
  95.4 20.6 %all-to-all-start.2 = ((bf16[128,1,1,64]{3,2,1,0:T(2,128)(2,1)}), bf16[128,1,1,64]{3,2,1,0:T(2,128)(2,1)S(1)}, u32[]{:S(2)}, u32[]{:S(2)}) async-start(bf16[128,1,1,64]{3,2,1,0:T(2,128)(2,1)} %copy.28), calls=%async_computation.2 | async-start | bytes 131072 | tf_op jit(solution)/shard_map/all_to_all | solution.py:125
  118.7 6.3 %collective-permute-start = (bf16[15,512]{1,0:T(8,128)(2,1)S(1)}, bf16[15,512]{1,0:T(8,128)(2,1)S(1)}, u32[]{:S(2)}, u32[]{:S(2)}) collective-permute-start(bf16[15,512]{1,0:T(8,128)(2,1)S(1)} %get-tuple-element.126), channel_id=1, source_target_pairs={{0,4},{4,8},{8,12},{12,16},{16,20},{20,24},{24,28},{28,32},{32,36}... | collective-permute-start | bytes 46088 | tf_op jit(solution)/shard_map/ppermute | solution.py:15
  123.0 7.2 %collective-permute-start.1 = (bf16[15,512]{1,0:T(8,128)(2,1)S(1)}, bf16[15,512]{1,0:T(8,128)(2,1)S(1)}, u32[]{:S(2)}, u32[]{:S(2)}) collective-permute-start(bf16[15,512]{1,0:T(8,128)(2,1)S(1)} %get-tuple-element.127), channel_id=1, source_target_pairs={{4,0},{8,4},{12,8},{16,12},{20,16},{24,20},{28,24},{32,28},{36,32}... | collective-permute-start | bytes 46088 | tf_op jit(solution)/shard_map/ppermute | solution.py:18
where the time goes:
time: 133 us; the launch traced here: 132 us
  waiting for transfers between devices  62.4 us (47%)
  starting transfers between devices  40.3 us (30%)
  other arithmetic  12.2 us (9%)
  matrix products  10.9 us (8%)
  local copies, waits for them, and re-layouts  5.18 us (4%)
    all_to_all x1, waiting for transfers between devices, on_device(): lax.all_to_all(paired, 'seq', split_axis=1, concat_axis=0, tiled=True)  32.1 us
    all_to_all x1, starting transfers between devices, on_device(): lax.all_to_all(queries.reshape(sub_rows, devices, columns), 'seq', split_...  19.7 us
    all_to_all x1, waiting for transfers between devices, on_device(): lax.all_to_all(context.reshape(devices, sub_rows, 1, columns), 'seq', spl...  13.4 us
    all_to_all x1, waiting for transfers between devices, on_device(): lax.all_to_all(queries.reshape(sub_rows, devices, columns), 'seq', split_...  11.7 us
    lt x16, other arithmetic, attend(): scores = jnp.where((key_frames < limit)[None, None, :], scores, -1e+30)  10.5 us
    all_to_all x1, starting transfers between devices, on_device(): lax.all_to_all(context.reshape(devices, sub_rows, 1, columns), 'seq', spl...  7.21 us
    all_to_all x1, starting transfers between devices, on_device(): lax.all_to_all(paired, 'seq', split_axis=1, concat_axis=0, tiled=True)  7.2 us
    ppermute x1, waiting for transfers between devices, extended(): lax.ppermute(lax.slice_in_dim(block, 0, width, axis=dim), axis, backward)  5.2 us
  transfers between devices with their start and end apart: 5, of which 4 were waited for; matrix products, arithmetic and copies ran while one was open for 1% of the time, Pallas kernels for 0%

commit v1 on v0

--- a/solution.py
+++ b/solution.py
@@ -90,8 +90,16 @@
     limit = lengths[0]
     local_frames = position * frames_here + jnp.arange(frames_here, dtype=jnp.int32)
     valid_local = (local_frames < limit).astype(jnp.float32)
-    query_rows = lax.all_to_all(
-        queries.reshape(sub_rows, devices, columns), "seq", split_axis=1, concat_axis=0, tiled=True
+    query_rows = jnp.concatenate(
+        lax.all_to_all(
+            jnp.stack(
+                jnp.split(queries.reshape(sub_rows, devices, columns), lax.axis_size("seq"), axis=1)
+            ),
+            "seq",
+            0,
+            0,
+        ),
+        axis=0,
     )
     carried = (
         jnp.full((heads_here, query_count), -1e30, jnp.float32),

time: 133 us -> 203 us (1.53)
  local copies, waits for them, and re-layouts: 5.18 us -> 74.7 us
    unnamed x14 -> x141, local copies, waits for them, and re-layouts: 0.03 us -> 69.6 us
where the time goes in v1:
time: 203 us; the launch traced here: 202 us
  local copies, waits for them, and re-layouts  74.7 us (37%)
  waiting for transfers between devices  62.4 us (31%)
  starting transfers between devices  40.3 us (20%)
  other arithmetic  12.2 us (6%)
  matrix products  10.9 us (5%)
    unnamed x141, local copies, waits for them, and re-layouts  69.6 us
    all_to_all x1, waiting for transfers between devices, on_device(): lax.all_to_all(paired, 'seq', split_axis=1, concat_axis=0, tiled=True)  32.1 us
    all_to_all x1, starting transfers between devices, on_device(): lax.all_to_all(jnp.stack(jnp.split(queries.reshape(sub_rows, devices, col...  19.7 us
    all_to_all x1, waiting for transfers between devices, on_device(): lax.all_to_all(context.reshape(devices, sub_rows, 1, columns), 'seq', spl...  13.4 us
    all_to_all x1, waiting for transfers between devices, on_device(): lax.all_to_all(jnp.stack(jnp.split(queries.reshape(sub_rows, devices, col...  11.7 us
    lt x16, other arithmetic, attend(): scores = jnp.where((key_frames < limit)[None, None, :], scores, -1e+30)  10.5 us
    all_to_all x1, starting transfers between devices, on_device(): lax.all_to_all(context.reshape(devices, sub_rows, 1, columns), 'seq', spl...  7.21 us
    all_to_all x1, starting transfers between devices, on_device(): lax.all_to_all(paired, 'seq', split_axis=1, concat_axis=0, tiled=True)  7.2 us
  transfers between devices with their start and end apart: 5, of which 4 were waited for; matrix products, arithmetic and copies ran while one was open for 1% of the time, Pallas kernels for 0%

profile of v1, /device:TPU:31, one launch (start us, length us, event | category | flops | bytes accessed | tf_op | source)
XLA Modules:
  0.0 202.0 jit_solution(96357215283600693)
XLA Ops:
  0.0 1.0 reshape.91
  71.2 19.7 %all-to-all-start.1 = ((bf16[128,1,1,64]{3,2,1,0:T(2,128)(2,1)}), bf16[128,1,1,64]{3,2,1,0:T(2,128)(2,1)S(1)}, u32[]{:S(2)}, u32[]{:S(2)}) async-start(bf16[128,1,1,64]{3,2,1,0:T(2,128)(2,1)} %constant_dynamic-update-slice_fusion), calls=%async_computation.1 | async-start | bytes 131072 | tf_op jit(solution)/shard_map/all_to_all | solution.py:94
  90.8 0.8 reshape.88
  91.7 0.8 reshape.89
  92.6 11.7 %all-to-all-done.1 = bf16[128,1,1,64]{3,2,1,0:T(2,128)(2,1)S(1)} async-done(((bf16[128,1,1,64]{3,2,1,0:T(2,128)(2,1)}), bf16[128,1,1,64]{3,2,1,0:T(2,128)(2,1)S(1)}, u32[]{:S(2)}, u32[]{:S(2)}) %all-to-all-start.1) | async-done | bytes 16416 | tf_op jit(solution)/shard_map/all_to_all | solution.py:94
  104.3 0.9 broadcast_in_dim.42
  105.2 7.2 %all-to-all-start = ((bf16[16,128,128]{2,0,1:T(8,128)(2,1)}), bf16[16,128,128]{2,0,1:T(8,128)(2,1)S(1)}, u32[]{:S(2)}, u32[]{:S(2)}) async-start(bf16[16,128,128]{2,0,1:T(8,128)(2,1)} %bitcast.11), calls=%async_computation | async-start | bytes 1048576 | tf_op jit(solution)/shard_map/all_to_all | solution.py:119
  113.2 32.1 %all-to-all-done = bf16[16,128,128]{2,0,1:T(8,128)(2,1)S(1)} async-done(((bf16[16,128,128]{2,0,1:T(8,128)(2,1)}), bf16[16,128,128]{2,0,1:T(8,128)(2,1)S(1)}, u32[]{:S(2)}, u32[]{:S(2)}) %all-to-all-start) | async-done | bytes 524320 | tf_op jit(solution)/shard_map/all_to_all | solution.py:119
  145.3 18.8 %while.14 = (s32[]{:T(128)}, f32[1,128]{1,0:T(1,128)S(1)}, f32[1,128]{1,0:T(1,128)S(1)}, f32[128,1,64]{0,2,1:T(8,128)S(1)}, s32[]{:T(128)}, /*index=5*/s32[]{:T(...) while((s32[]{:T(128)}, f32[1,128]{1,0:T(1,128)S(1)}, ...), condition=%wide.region_3.4_spmd, body=%wide.region_0.3_spmd.sunk | while | flops 4326023 | bytes 353099 | solution.py:130
  145.3 0.7 add_compare_fusion.2
  146.5 0.7 add_compare_fusion.2
  147.7 0.7 add_compare_fusion.2
  148.9 0.7 add_compare_fusion.2
  150.1 0.7 add_compare_fusion.2
  151.2 0.7 add_compare_fusion.2
  152.4 0.7 add_compare_fusion.2
  153.6 0.7 add_compare_fusion.2
  154.8 0.7 add_compare_fusion.2
  155.9 0.7 add_compare_fusion.2
  157.1 0.7 add_compare_fusion.2
  158.3 0.7 add_compare_fusion.2
  160.6 0.7 add_compare_fusion.2
  161.8 0.7 add_compare_fusion.2
  163.0 0.7 add_compare_fusion.2
  164.2 0.7 copy.418
  164.9 7.2 %all-to-all-start.2 = ((bf16[128,1,1,64]{3,2,1,0:T(2,128)(2,1)}), bf16[128,1,1,64]{3,2,1,0:T(2,128)(2,1)S(1)}, u32[]{:S(2)}, u32[]{:S(2)}) async-start(bf16[128,1,1,64]{3,2,1,0:T(2,128)(2,1)} %copy.418), calls=%async_computation.2 | async-start | bytes 131072 | tf_op jit(solution)/shard_map/all_to_all | solution.py:133
  172.1 13.4 %all-to-all-done.2 = bf16[128,1,1,64]{3,2,1,0:T(2,128)(2,1)S(1)} async-done(((bf16[128,1,1,64]{3,2,1,0:T(2,128)(2,1)}), bf16[128,1,1,64]{3,2,1,0:T(2,128)(2,1)S(1)}, u32[]{:S(2)}, u32[]{:S(2)}) %all-to-all-start.2) | async-done | bytes 16416 | tf_op jit(solution)/shard_map/all_to_all | solution.py:133
  185.8 1.6 fusion.94
  188.2 4.3 %collective-permute-start = (bf16[15,512]{1,0:T(8,128)(2,1)S(1)}, bf16[15,512]{1,0:T(8,128)(2,1)S(1)}, u32[]{:S(2)}, u32[]{:S(2)}) collective-permute-start(bf16[15,512]{1,0:T(8,128)(2,1)S(1)} %get-tuple-element.150), channel_id=1, source_target_pairs={{0,4},{4,8},{8,12},{12,16},{16,20},{20,24},{24,28},{28,32},{32,36}... | collective-permute-start | bytes 46088 | tf_op jit(solution)/shard_map/ppermute | solution.py:15
  192.5 1.9 collective-permute-start.1
  194.5 5.2 %collective-permute-done.1 = bf16[15,512]{1,0:T(8,128)(2,1)S(1)} collective-permute-done((bf16[15,512]{1,0:T(8,128)(2,1)S(1)}, bf16[15,512]{1,0:T(8,128)(2,1)S(1)}, u32[]{:S(2)}, u32[]{:S(2)}) %collective-permute-start.1) | collective-permute-done | bytes 15392 | tf_op jit(solution)/shard_map/ppermute | solution.py:18
  199.7 2.3 %fusion.11 = bf16[16,1024]{1,0:T(8,128)(2,1)} fusion(f32[16,1024]{1,0:T(8,128)S(1)} %get-tuple-element.153, bf16[512,1024]{1,0:T(8,128)(2,1)} %param.27, f32[46,512]{1,0:T(8,128)S(1)} %maximum_convert_fusion, f32[512]{0:T(512)S(1)} %copy-done.5, f32[512]{0:T(512)S(1)} %copy-done.6, f32[512]{0:T(512)S(1)} %bitcast.640, f32[512]{0:T(512)S(1)} %bitcast.641, ...), kind=kOutput, calls=%fused_computation.21 | convolution fusion | flops 17367040 | bytes 2230272 | tf_op jit(solution)/shard_map/dot_general | solution.py:153
  (260 shorter events, 79.8 us)
Async XLA Ops:
  0.0 187.7 %copy-start = (bf16[1024,1024]{1,0:T(8,128)(2,1)S(1)}, bf16[1024,1024]{1,0:T(8,128)(2,1)}, u32[]{:S(2)}) copy-start(bf16[1024,1024]{1,0:T(8,128)(2,1)} %param.23) | copy-start | bytes 6291460
  0.0 113.1 %copy-start.1 = (f32[31,512]{1,0:T(8,128)S(1)}, f32[31,512]{1,0:T(8,128)}, u32[]{:S(2)}) copy-start(f32[31,512]{1,0:T(8,128)} %param.24) | copy-start | bytes 190468
  71.2 33.1 %all-to-all-start.1 = ((bf16[128,1,1,64]{3,2,1,0:T(2,128)(2,1)}), bf16[128,1,1,64]{3,2,1,0:T(2,128)(2,1)S(1)}, u32[]{:S(2)}, u32[]{:S(2)}) async-start(bf16[128,1,1,64]{3,2,1,0:T(2,128)(2,1)} %constant_dynamic-update-slice_fusion), calls=%async_computation.1 | async-start | bytes 131072 | tf_op jit(solution)/shard_map/all_to_all | solution.py:94
  92.6 93.3 %copy-start.2 = (bf16[16,1024]{1,0:T(8,128)(2,1)S(1)}, bf16[16,1024]{1,0:T(8,128)(2,1)}, u32[]{:S(2)}) copy-start(bf16[16,1024]{1,0:T(8,128)(2,1)} %param.18) | copy-start | bytes 98308
  105.2 40.2 %all-to-all-start = ((bf16[16,128,128]{2,0,1:T(8,128)(2,1)}), bf16[16,128,128]{2,0,1:T(8,128)(2,1)S(1)}, u32[]{:S(2)}, u32[]{:S(2)}) async-start(bf16[16,128,128]{2,0,1:T(8,128)(2,1)} %bitcast.11), calls=%async_computation | async-start | bytes 1048576 | tf_op jit(solution)/shard_map/all_to_all | solution.py:119
  112.4 75.3 %copy-start.3 = (f32[1024]{0:T(1024)S(1)}, f32[1024]{0:T(1024)}, u32[]{:S(2)}) copy-start(f32[1024]{0:T(1024)} %param.22) | copy-start | bytes 12292
  112.4 75.3 %copy-start.4 = (f32[1024]{0:T(1024)S(1)}, f32[1024]{0:T(1024)}, u32[]{:S(2)}) copy-start(f32[1024]{0:T(1024)} %param.21) | copy-start | bytes 12292
  164.9 34.8 %copy-start.5 = (f32[512]{0:T(512)S(1)}, f32[512]{0:T(512)}, u32[]{:S(2)}) copy-start(f32[512]{0:T(512)} %param.26) | copy-start | bytes 6148
  164.9 34.8 %copy-start.6 = (f32[512]{0:T(512)S(1)}, f32[512]{0:T(512)}, u32[]{:S(2)}) copy-start(f32[512]{0:T(512)} %param.25) | copy-start | bytes 6148
  164.9 20.6 %all-to-all-start.2 = ((bf16[128,1,1,64]{3,2,1,0:T(2,128)(2,1)}), bf16[128,1,1,64]{3,2,1,0:T(2,128)(2,1)S(1)}, u32[]{:S(2)}, u32[]{:S(2)}) async-start(bf16[128,1,1,64]{3,2,1,0:T(2,128)(2,1)} %copy.418), calls=%async_computation.2 | async-start | bytes 131072 | tf_op jit(solution)/shard_map/all_to_all | solution.py:133
  188.2 6.3 %collective-permute-start = (bf16[15,512]{1,0:T(8,128)(2,1)S(1)}, bf16[15,512]{1,0:T(8,128)(2,1)S(1)}, u32[]{:S(2)}, u32[]{:S(2)}) collective-permute-start(bf16[15,512]{1,0:T(8,128)(2,1)S(1)} %get-tuple-element.150), channel_id=1, source_target_pairs={{0,4},{4,8},{8,12},{12,16},{16,20},{20,24},{24,28},{28,32},{32,36}... | collective-permute-start | bytes 46088 | tf_op jit(solution)/shard_map/ppermute | solution.py:15
  192.5 7.2 %collective-permute-start.1 = (bf16[15,512]{1,0:T(8,128)(2,1)S(1)}, bf16[15,512]{1,0:T(8,128)(2,1)S(1)}, u32[]{:S(2)}, u32[]{:S(2)}) collective-permute-start(bf16[15,512]{1,0:T(8,128)(2,1)S(1)} %get-tuple-element.151), channel_id=1, source_target_pairs={{4,0},{8,4},{12,8},{16,12},{20,16},{24,20},{28,24},{32,28},{36,32}... | collective-permute-start | bytes 46088 | tf_op jit(solution)/shard_map/ppermute | solution.py:18
